TPU v7x, 32 devices: a whole 2x2x4 slice. The times are simulated.
32 devices in a mesh: section: 2 (over x), dp: 16 (over z, y, core).
Axes of the slice: x: 2, y: 2, z: 4, core: 2. Of those that a mesh axis runs over, the one named last changes fastest.
Arguments:
- section_inputs: bfloat16 [2, 2048, 8192], P('section', 'dp'), may hold values from -6 to 6
- teacher_states: bfloat16 [2048, 8192], P('dp'), may hold values from -6 to 6
- confidence: int32 [2048], P('dp'), may hold values from 1 to 256
- gains: float32 [2, 8192], P('section'), may hold values from 0.1 to 1.9
- w_down: bfloat16 [2, 8192, 256], P('section', 'dp'), may hold values from -0.0625 to 0.0625
- w_up: bfloat16 [2, 8192, 256], P('section', 'dp'), may hold values from -0.375 to 0.375
Outputs:
- input_grads: bfloat16 [2, 2048, 8192], P('section', 'dp')
- grad_down: float32 [2, 8192, 256], P('section', 'dp')
- grad_up: float32 [2, 8192, 256], P('section', 'dp')
- grad_gain: float32 [2, 8192], P('section', 'dp')
All inputs are finite; a program needn't handle non-finite values.
Results may differ from a plain program's by a relative error of at most 0.013.
Values may be sent and summed in bfloat16 or wider, within the bound.
No kernel may reach another device: no remote copies, remote signals or barrier semaphores. Data moves between devices by JAX's collectives and lax.ppermute only.
A program may use at most 64 MiB of HBM per device.

v0:
```python
import jax
import jax.numpy as jnp
from jax import lax
from jax.sharding import PartitionSpec as P

MICRO = 4
ROWS = 32
TOK_DEV = 128
EPSILON = 1e-05


def shifted(block, axis, distance):
    devices = range(lax.axis_size(axis))
    route = [(i - distance, i) for i in devices if i - distance in devices]
    return lax.ppermute(block, axis, route)


def write_rows(buffer, fresh, first_row, active_step):
    previous = lax.dynamic_slice_in_dim(buffer, first_row, fresh.shape[0], 0)
    return lax.dynamic_update_slice_in_dim(
        buffer, jnp.where(active_step, fresh, previous), first_row, 0
    )


def local(section_inputs, teacher_states, confidence, gains, w_down, w_up):
    sections = lax.axis_size("section")
    section_index = lax.axis_index("section")
    layer_inputs = section_inputs[0]
    gain = gains[0]
    down_matrix, up_matrix = (
        lax.all_gather(w_down[0], "dp", axis=0, tiled=True),
        lax.all_gather(w_up[0], "dp", axis=0, tiled=True),
    )
    is_last = section_index == sections - 1
    rank_width = down_matrix.shape[1]
    width = down_matrix.shape[0]

    def run_step(step_index, carry):
        incoming, scaled_all, cot_all, pre_all, hidden_all, grads_all, gain_term = carry
        micro_index = step_index - (sections - 1 - section_index)
        active_step = (micro_index >= 0) & (micro_index < MICRO)
        first_row = jnp.clip(micro_index, 0, MICRO - 1) * ROWS
        rows_in = lax.dynamic_slice_in_dim(layer_inputs, first_row, ROWS, 0)
        teacher_rows = lax.dynamic_slice_in_dim(teacher_states, first_row, ROWS, 0)
        weight_rows = (
            lax.dynamic_slice_in_dim(confidence, first_row, ROWS, 0).astype(jnp.float32) / 256.0
        )
        values = rows_in.astype(jnp.float32)
        inverse = lax.rsqrt(jnp.mean(values * values, axis=-1, keepdims=True) + EPSILON)
        normed = values * inverse
        scaled = (normed * gain).astype(jnp.bfloat16)
        preact = jnp.dot(scaled, down_matrix, preferred_element_type=jnp.float32)
        hidden = jax.nn.silu(preact).astype(jnp.bfloat16)
        branch = jnp.einsum("tr,dr->td", hidden, up_matrix, preferred_element_type=jnp.float32)
        top_grad = (
            weight_rows[:, None] * (values + branch - teacher_rows.astype(jnp.float32))
        ).astype(jnp.bfloat16)
        cotangent = jnp.where(is_last, top_grad, incoming)
        hidden_grad = jnp.dot(cotangent, up_matrix, preferred_element_type=jnp.float32)
        sigmoid_val = jax.nn.sigmoid(preact)
        pre_grad = (hidden_grad * sigmoid_val * (1.0 + preact * (1.0 - sigmoid_val))).astype(
            jnp.bfloat16
        )
        normed_grad = jnp.einsum(
            "tr,dr->td", pre_grad, down_matrix, preferred_element_type=jnp.float32
        )
        scaled_grad = normed_grad * gain
        input_grad = cotangent.astype(jnp.float32) + inverse * (
            scaled_grad - normed * jnp.mean(scaled_grad * normed, axis=-1, keepdims=True)
        )
        input_grad = input_grad.astype(jnp.bfloat16)
        gain_term = gain_term + jnp.where(active_step, jnp.sum(normed_grad * normed, axis=0), 0.0)
        scaled_all = write_rows(scaled_all, scaled, first_row, active_step)
        cot_all = write_rows(cot_all, cotangent, first_row, active_step)
        pre_all = write_rows(pre_all, pre_grad, first_row, active_step)
        hidden_all = write_rows(hidden_all, hidden, first_row, active_step)
        grads_all = write_rows(grads_all, input_grad, first_row, active_step)
        outgoing = shifted(input_grad, "section", -1)
        return (outgoing, scaled_all, cot_all, pre_all, hidden_all, grads_all, gain_term)

    token_count = layer_inputs.shape[0]
    start_carry = (
        jnp.zeros((ROWS, width), jnp.bfloat16),
        jnp.zeros((token_count, width), jnp.bfloat16),
        jnp.zeros((token_count, width), jnp.bfloat16),
        jnp.zeros((token_count, rank_width), jnp.bfloat16),
        jnp.zeros((token_count, rank_width), jnp.bfloat16),
        jnp.zeros((token_count, width), jnp.bfloat16),
        jnp.zeros((width,), jnp.float32),
    )
    final_carry = lax.fori_loop(0, MICRO + sections - 1, run_step, start_carry)
    _, scaled_all, cot_all, pre_all, hidden_all, grads_all, gain_term = final_carry
    down_part = jnp.einsum("td,tr->dr", scaled_all, pre_all, preferred_element_type=jnp.float32)
    up_part = jnp.einsum("td,tr->dr", cot_all, hidden_all, preferred_element_type=jnp.float32)
    stacked = lax.psum_scatter(
        jnp.concatenate([down_part, up_part], axis=1).astype(jnp.bfloat16),
        "dp",
        scatter_dimension=0,
        tiled=True,
    ).astype(jnp.float32)
    gain_sum = lax.psum_scatter(gain_term, "dp", scatter_dimension=0, tiled=True)
    stacked = stacked / TOK_DEV
    grad_down = stacked[:, :rank_width]
    grad_up = stacked[:, rank_width:]
    return (grads_all[None], grad_down[None], grad_up[None], (gain_sum / TOK_DEV)[None])


def solution(mesh):
    in_specs = (
        P("section", "dp", None),
        P("dp", None),
        P("dp"),
        P("section", None),
        P("section", "dp", None),
        P("section", "dp", None),
    )
    out_specs = (
        P("section", "dp", None),
        P("section", "dp", None),
        P("section", "dp", None),
        P("section", "dp"),
    )
    return jax.shard_map(local, mesh=mesh, in_specs=in_specs, out_specs=out_specs, check_vma=False)
```

profile of v0, /device:TPU:0, one launch (start us, length us, event | category | flops | bytes accessed | tf_op | source)
XLA Modules:
  0.0 383.3 jit_solution(15505079731274536532)
XLA Ops:
  8.7 54.7 %all-gather.5.cloned.1.call-done = bf16[1,8192,256]{2,1,0:T(8,128)(2,1)} async-done(((bf16[1,512,256]{2,1,0:T(8,128)(2,1)}), bf16[1,8192,256]{2,1,0:T(8,128)(2,1)}) %all-gather.5.cloned.1.call-update) | async-done | bytes 4194320 | tf_op jit(solution)/shard_map/all_gather | solution.py:31
  63.5 51.2 %all-gather.7.cloned.1.call-done = bf16[1,8192,256]{2,1,0:T(8,128)(2,1)} async-done(((bf16[1,512,256]{2,1,0:T(8,128)(2,1)}), bf16[1,8192,256]{2,1,0:T(8,128)(2,1)}) %all-gather.7.cloned.1.call-update) | async-done | bytes 4194320 | tf_op jit(solution)/shard_map/all_gather | solution.py:32
  119.3 135.4 %while.28 = (s32[]{:T(128)}, bf16[32,8192]{1,0:T(8,128)(2,1)S(1)}, bf16[128,8192]{1,0:T(8,128)(2,1)}, bf16[128,8192]{1,0:T(8,128)(2,1)}, bf16[128,256]{1,0:T(8,1...) while((s32[]{:T(128)}, bf16[32,8192]{1,0:T(8,128)(2,1)S(1)}, ...), condition=%wide.region_4.5_spmd.clone, body=%wide.region_0.4_spmd.clone.sunk | while | flops 546234496 | bytes 63868848 | solution.py:91
  119.7 3.2 select_dynamic-update-slice_fusion.8
  129.2 3.0 select_dynamic-update-slice_fusion.10
  133.5 14.7 %collective-permute-done = bf16[32,8192]{1,0:T(8,128)(2,1)S(1)} collective-permute-done((bf16[32,8192]{1,0:T(8,128)(2,1)S(1)}, bf16[32,8192]{1,0:T(8,128)(2,1)S(1)}, u32[]{:S(2)}, u32[]{:S(2)}) %collective-permute-start) | collective-permute-done | bytes 524320 | tf_op jit(solution)/shard_map/while/body/eval_jaxpr/ppermute | solution.py:15
  148.5 3.2 select_dynamic-update-slice_fusion.8
  158.1 3.0 select_dynamic-update-slice_fusion.10
  162.4 13.8 %collective-permute-done = bf16[32,8192]{1,0:T(8,128)(2,1)S(1)} collective-permute-done((bf16[32,8192]{1,0:T(8,128)(2,1)S(1)}, bf16[32,8192]{1,0:T(8,128)(2,1)S(1)}, u32[]{:S(2)}, u32[]{:S(2)}) %collective-permute-start) | collective-permute-done | bytes 524320 | tf_op jit(solution)/shard_map/while/body/eval_jaxpr/ppermute | solution.py:15
  176.6 3.2 select_dynamic-update-slice_fusion.8
  186.1 3.0 select_dynamic-update-slice_fusion.10
  190.4 12.9 %collective-permute-done = bf16[32,8192]{1,0:T(8,128)(2,1)S(1)} collective-permute-done((bf16[32,8192]{1,0:T(8,128)(2,1)S(1)}, bf16[32,8192]{1,0:T(8,128)(2,1)S(1)}, u32[]{:S(2)}, u32[]{:S(2)}) %collective-permute-start) | collective-permute-done | bytes 524320 | tf_op jit(solution)/shard_map/while/body/eval_jaxpr/ppermute | solution.py:15
  203.7 3.2 select_dynamic-update-slice_fusion.8
  213.2 3.0 select_dynamic-update-slice_fusion.10
  217.5 12.0 %collective-permute-done = bf16[32,8192]{1,0:T(8,128)(2,1)S(1)} collective-permute-done((bf16[32,8192]{1,0:T(8,128)(2,1)S(1)}, bf16[32,8192]{1,0:T(8,128)(2,1)S(1)}, u32[]{:S(2)}, u32[]{:S(2)}) %collective-permute-start) | collective-permute-done | bytes 524320 | tf_op jit(solution)/shard_map/while/body/eval_jaxpr/ppermute | solution.py:15
  229.8 3.2 select_dynamic-update-slice_fusion.8
  233.3 2.4 fusion.48
  239.3 3.0 select_dynamic-update-slice_fusion.10
  243.7 11.1 %collective-permute-done = bf16[32,8192]{1,0:T(8,128)(2,1)S(1)} collective-permute-done((bf16[32,8192]{1,0:T(8,128)(2,1)S(1)}, bf16[32,8192]{1,0:T(8,128)(2,1)S(1)}, u32[]{:S(2)}, u32[]{:S(2)}) %collective-permute-start) | collective-permute-done | bytes 524320 | tf_op jit(solution)/shard_map/while/body/eval_jaxpr/ppermute | solution.py:15
  254.8 5.0 %convolution_convert_fusion.1 = bf16[8192,256]{0,1:T(8,128)(2,1)} fusion(bf16[128,8192]{1,0:T(8,128)(2,1)} %get-tuple-element.369, bf16[128,256]{1,0:T(8,128)(2,1)S(1)} %get-tuple-element.370), kind=kOutput, calls=%fused_computation.36 | convolution fusion | flops 538968064 | bytes 6356992 | tf_op jit(solution)/shard_map/td,tr->dr/dot_general | solution.py:93
  259.7 3.2 convolution_convert_fusion
  263.0 7.7 %pad_maximum_fusion = bf16[8192,512]{0,1:T(8,128)(2,1)} fusion(bf16[8192,256]{0,1:T(8,128)(2,1)} %convolution_convert_fusion, bf16[8192,256]{0,1:T(8,128)(2,1)} %convolution_convert_fusion.1), kind=kLoop, calls=%fused_computation.37 | loop fusion | flops 16777216 | bytes 16777216 | tf_op jit(solution)/shard_map/concatenate | solution.py:96
  272.5 59.9 %all-reduce = f32[8192]{0:T(1024)S(1)} all-reduce(f32[8192]{0:T(1024)S(1)} %get-tuple-element.373), channel_id=5, replica_groups=mesh['section'=2,'dp'=16] {'dp'}, use_global_device_ids=true, to_apply=%region_6.7.clone | all-reduce | flops 8192 | bytes 65536
  333.1 40.4 %reduce-scatter.2.cloned.1.call-done = bf16[512,512]{0,1:T(8,128)(2,1)} async-done(((bf16[8192,512]{0,1:T(8,128)(2,1)}), bf16[512,512]{0,1:T(8,128)(2,1)}) %reduce-scatter.2.cloned.1.call-update) | async-done | bytes 524304 | tf_op jit(solution)/shard_map/reduce_scatter | solution.py:95
  (93 shorter events, 48.2 us)
Async XLA Ops:
  7.2 56.3 %all-gather.5.cloned.1.call-start = ((), (), s32[]{:S(2)}) async-start(), calls=%async_computation.2 | async-start | bytes 4456448 | tf_op jit(solution)/shard_map/all_gather | solution.py:31
  7.9 106.8 %all-gather.7.cloned.1.call-start = ((), (), s32[]{:S(2)}) async-start(), calls=%async_computation.3 | async-start | bytes 4456448 | tf_op jit(solution)/shard_map/all_gather | solution.py:32
  8.6 364.9 %reduce-scatter.2.cloned.1.call-start = ((), (), s32[]{:S(2)}) async-start(), calls=%async_computation.1 | async-start | bytes 8912896 | tf_op jit(solution)/shard_map/reduce_scatter | solution.py:95
  116.3 3.0 copy-start.2
  116.3 3.0 copy-start.4
  116.3 3.0 copy-start.5
  119.7 3.5 copy-start.1
  125.6 2.2 copy-start
  132.2 16.0 %collective-permute-start = (bf16[32,8192]{1,0:T(8,128)(2,1)S(1)}, bf16[32,8192]{1,0:T(8,128)(2,1)S(1)}, u32[]{:S(2)}, u32[]{:S(2)}) collective-permute-start(bf16[32,8192]{1,0:T(8,128)(2,1)S(1)} %get-tuple-element.590), channel_id=1, source_target_pairs={{16,0},{17,1},{18,2},{19,3},{20,4},{21,5},{22,6},{23,7},{24,8},{25... | collective-permute-start | bytes 1572872 | tf_op jit(solution)/shard_map/while/body/eval_jaxpr/ppermute | solution.py:15
  148.5 3.5 copy-start.1
  154.4 2.2 copy-start
  161.1 15.2 %collective-permute-start = (bf16[32,8192]{1,0:T(8,128)(2,1)S(1)}, bf16[32,8192]{1,0:T(8,128)(2,1)S(1)}, u32[]{:S(2)}, u32[]{:S(2)}) collective-permute-start(bf16[32,8192]{1,0:T(8,128)(2,1)S(1)} %get-tuple-element.590), channel_id=1, source_target_pairs={{16,0},{17,1},{18,2},{19,3},{20,4},{21,5},{22,6},{23,7},{24,8},{25... | collective-permute-start | bytes 1572872 | tf_op jit(solution)/shard_map/while/body/eval_jaxpr/ppermute | solution.py:15
  176.5 3.5 copy-start.1
  182.4 2.2 copy-start
  189.1 14.2 %collective-permute-start = (bf16[32,8192]{1,0:T(8,128)(2,1)S(1)}, bf16[32,8192]{1,0:T(8,128)(2,1)S(1)}, u32[]{:S(2)}, u32[]{:S(2)}) collective-permute-start(bf16[32,8192]{1,0:T(8,128)(2,1)S(1)} %get-tuple-element.590), channel_id=1, source_target_pairs={{16,0},{17,1},{18,2},{19,3},{20,4},{21,5},{22,6},{23,7},{24,8},{25... | collective-permute-start | bytes 1572872 | tf_op jit(solution)/shard_map/while/body/eval_jaxpr/ppermute | solution.py:15
  203.6 3.5 copy-start.1
  209.5 2.2 copy-start
  216.2 13.3 %collective-permute-start = (bf16[32,8192]{1,0:T(8,128)(2,1)S(1)}, bf16[32,8192]{1,0:T(8,128)(2,1)S(1)}, u32[]{:S(2)}, u32[]{:S(2)}) collective-permute-start(bf16[32,8192]{1,0:T(8,128)(2,1)S(1)} %get-tuple-element.590), channel_id=1, source_target_pairs={{16,0},{17,1},{18,2},{19,3},{20,4},{21,5},{22,6},{23,7},{24,8},{25... | collective-permute-start | bytes 1572872 | tf_op jit(solution)/shard_map/while/body/eval_jaxpr/ppermute | solution.py:15
  229.8 3.5 copy-start.1
  235.7 2.2 copy-start
  242.4 12.4 %collective-permute-start = (bf16[32,8192]{1,0:T(8,128)(2,1)S(1)}, bf16[32,8192]{1,0:T(8,128)(2,1)S(1)}, u32[]{:S(2)}, u32[]{:S(2)}) collective-permute-start(bf16[32,8192]{1,0:T(8,128)(2,1)S(1)} %get-tuple-element.590), channel_id=1, source_target_pairs={{16,0},{17,1},{18,2},{19,3},{20,4},{21,5},{22,6},{23,7},{24,8},{25... | collective-permute-start | bytes 1572872 | tf_op jit(solution)/shard_map/while/body/eval_jaxpr/ppermute | solution.py:15
  254.8 5.0 %copy-start.3 = (bf16[128,8192]{1,0:T(8,128)(2,1)S(1)}, bf16[128,8192]{1,0:T(8,128)(2,1)}, u32[]{:S(2)}) copy-start(bf16[128,8192]{1,0:T(8,128)(2,1)} %get-tuple-element.371) | copy-start | bytes 6291460
  270.7 0.7 copy-start.6
Sparse Core Ops, SparseCore 0:
  10.2 53.2 all-gather.4
  65.6 49.0 all-gather.6
  270.8 102.6 reduce-scatter.1
where the time goes:
time: 384 us; the launch traced here: 383 us
  waiting for transfers between devices  212 us (55%)
  blocking collectives  59.9 us (16%)
  matrix products  47.9 us (12%)
  other arithmetic  26.3 us (7%)
  local copies, waits for them, and re-layouts  15.7 us (4%)
  between operations  14.5 us (4%)
  starting transfers between devices  6.52 us (2%)
    ppermute x5, waiting for transfers between devices, shifted(): return lax.ppermute(block, axis, route)  64.5 us
    unnamed x1, blocking collectives  59.9 us
    all_gather x1, waiting for transfers between devices, local(): lax.all_gather(w_down[0], 'dp', axis=0, tiled=True)  54.7 us
    all_gather x1, waiting for transfers between devices, local(): lax.all_gather(w_up[0], 'dp', axis=0, tiled=True)  51.2 us
    reduce_scatter x1, waiting for transfers between devices, local(): lax.psum_scatter(jnp.concatenate([down_part, up_part], axis=1).astype(jnp...  40.4 us
    dot_general x5, matrix products, run_step(): preact = jnp.dot(scaled, down_matrix, preferred_element_type=jnp.float32)  16.2 us
    dynamic_update_slice x5, other arithmetic, write_rows(): lax.dynamic_update_slice_in_dim(buffer, jnp.where(active_step, fresh, pre...  15.1 us
    dot_general x5, matrix products, run_step(): jnp.einsum('tr,dr->td', hidden, up_matrix, preferred_element_type=jnp.flo...  12 us
  transfers between devices with their start and end apart: 8, of which 8 were waited for; matrix products, arithmetic and copies ran while one was open for 0% of the time, Pallas kernels for 0%

commit v1 on v0

--- a/solution.py
+++ b/solution.py
@@ -7,6 +7,28 @@
 ROWS = 32
 TOK_DEV = 128
 EPSILON = 1e-05
+
+
+def in_order(tiles, dim):
+    tiles = jnp.moveaxis(tiles, 0, dim)
+    lengths = tiles.shape
+    return tiles.reshape(*lengths[:dim], lengths[dim] * lengths[dim + 1], *lengths[dim + 2 :])
+
+
+def collected_by_bits(x, axis):
+    size = lax.axis_size(axis)
+    pieces = x[None]
+    for level in range(size.bit_length() - 1):
+        bit = 1 << level
+        received = lax.ppermute(pieces, axis, [(i, i ^ bit) for i in range(size)])
+        both = jnp.stack([pieces, received])
+        upper = lax.axis_index(axis) >> level & 1
+        pieces = jnp.where(upper == 0, both, both[::-1]).reshape(-1, *x.shape)
+    return pieces
+
+
+def gather_by_bits(x, axis, dim):
+    return in_order(collected_by_bits(x, axis), dim)
 
 
 def shifted(block, axis, distance):
@@ -29,7 +51,7 @@
     gain = gains[0]
     down_matrix, up_matrix = (
         lax.all_gather(w_down[0], "dp", axis=0, tiled=True),
-        lax.all_gather(w_up[0], "dp", axis=0, tiled=True),
+        gather_by_bits(w_up[0], "dp", 0),
     )
     is_last = section_index == sections - 1
     rank_width = down_matrix.shape[1]

time: 384 us -> 442 us (1.15)
  waiting for transfers between devices: 212 us -> 257 us
  other arithmetic: 26.3 us -> 33.3 us
  starting transfers between devices: 6.52 us -> 12.5 us
    ppermute x0 -> x4, waiting for transfers between devices: none -> 152 us  [collected_by_bits(): received = lax.ppermute(pieces, axis, [(i, i ^ bit) for i in range(size)])]
    all_gather x1, waiting for transfers between devices: 54.7 us -> 0.01 us  [local(): lax.all_gather(w_down[0], 'dp', axis=0, tiled=True)]
    all_gather x1 -> x0, waiting for transfers between devices: 51.2 us -> none  [local(): lax.all_gather(w_up[0], 'dp', axis=0, tiled=True)]
    ppermute x0 -> x4, starting transfers between devices: none -> 6.04 us  [collected_by_bits(): received = lax.ppermute(pieces, axis, [(i, i ^ bit) for i in range(size)])]
  transfers between devices with their start and end apart: 8 -> 11, of which waited for: 8 -> 10; matrix products, arithmetic and copies ran while one was open for 0% -> 2% of each run, Pallas kernels for 0% -> 0%
where the time goes in v1:
time: 442 us; the launch traced here: 441 us
  waiting for transfers between devices  257 us (58%)
  blocking collectives  59.5 us (13%)
  matrix products  47.9 us (11%)
  other arithmetic  33.3 us (8%)
  local copies, waits for them, and re-layouts  15.7 us (4%)
  between operations  14.8 us (3%)
  starting transfers between devices  12.5 us (3%)
    ppermute x4, waiting for transfers between devices, collected_by_bits(): received = lax.ppermute(pieces, axis, [(i, i ^ bit) for i in range(size)])  152 us
    ppermute x5, waiting for transfers between devices, shifted(): return lax.ppermute(block, axis, route)  62.9 us
    unnamed x1, blocking collectives  59.5 us
    reduce_scatter x1, waiting for transfers between devices, local(): lax.psum_scatter(jnp.concatenate([down_part, up_part], axis=1).astype(jnp...  41.4 us
    dot_general x5, matrix products, run_step(): preact = jnp.dot(scaled, down_matrix, preferred_element_type=jnp.float32)  16.2 us
    dynamic_update_slice x5, other arithmetic, write_rows(): lax.dynamic_update_slice_in_dim(buffer, jnp.where(active_step, fresh, pre...  15.1 us
    dot_general x5, matrix products, run_step(): jnp.einsum('tr,dr->td', hidden, up_matrix, preferred_element_type=jnp.flo...  12 us
  transfers between devices with their start and end apart: 11, of which 10 were waited for; matrix products, arithmetic and copies ran while one was open for 2% of the time, Pallas kernels for 0%

profile of v1, /device:TPU:0, one launch (start us, length us, event | category | flops | bytes accessed | tf_op | source)
XLA Modules:
  0.0 440.8 jit_solution(8160343938024361907)
XLA Ops:
  13.9 15.0 %collective-permute-done.2 = bf16[2,512,256]{2,1,0:T(8,128)(2,1)S(1)} collective-permute-done((bf16[2,512,256]{2,1,0:T(8,128)(2,1)S(1)}, bf16[2,512,256]{2,1,0:T(8,128)(2,1)S(1)}, u32[]{:S(2)}, u32[]{:S(2)}) %collective-permute-start.2) | collective-permute-done | bytes 524320 | tf_op jit(solution)/shard_map/ppermute | solution.py:23
  31.1 43.2 %collective-permute-done.3 = bf16[4,512,256]{2,1,0:T(8,128)(2,1)S(1)} collective-permute-done((bf16[4,512,256]{2,1,0:T(8,128)(2,1)S(1)}, bf16[4,512,256]{2,1,0:T(8,128)(2,1)S(1)}, u32[]{:S(2)}, u32[]{:S(2)}) %collective-permute-start.3) | collective-permute-done | bytes 1048608 | tf_op jit(solution)/shard_map/ppermute | solution.py:23
  75.7 92.3 %collective-permute-done.4 = bf16[8,512,256]{2,1,0:T(8,128)(2,1)} collective-permute-done((bf16[8,512,256]{2,1,0:T(8,128)(2,1)S(1)}, bf16[8,512,256]{2,1,0:T(8,128)(2,1)}, u32[]{:S(2)}, u32[]{:S(2)}) %collective-permute-start.4) | collective-permute-done | bytes 2097184 | tf_op jit(solution)/shard_map/ppermute | solution.py:23
  177.6 133.8 %while.28 = (s32[]{:T(128)}, bf16[32,8192]{1,0:T(8,128)(2,1)S(1)}, bf16[128,8192]{1,0:T(8,128)(2,1)}, bf16[128,8192]{1,0:T(8,128)(2,1)}, bf16[128,256]{1,0:T(8,1...) while((s32[]{:T(128)}, bf16[32,8192]{1,0:T(8,128)(2,1)S(1)}, ...), condition=%wide.region_4.5_spmd.clone, body=%wide.region_0.4_spmd.clone.sunk | while | flops 546234496 | bytes 63868848 | solution.py:113
  178.0 3.2 select_dynamic-update-slice_fusion.8
  187.5 3.0 select_dynamic-update-slice_fusion.10
  191.8 14.4 %collective-permute-done = bf16[32,8192]{1,0:T(8,128)(2,1)S(1)} collective-permute-done((bf16[32,8192]{1,0:T(8,128)(2,1)S(1)}, bf16[32,8192]{1,0:T(8,128)(2,1)S(1)}, u32[]{:S(2)}, u32[]{:S(2)}) %collective-permute-start) | collective-permute-done | bytes 524320 | tf_op jit(solution)/shard_map/while/body/eval_jaxpr/ppermute | solution.py:37
  206.5 3.2 select_dynamic-update-slice_fusion.8
  216.0 3.0 select_dynamic-update-slice_fusion.10
  220.4 13.5 %collective-permute-done = bf16[32,8192]{1,0:T(8,128)(2,1)S(1)} collective-permute-done((bf16[32,8192]{1,0:T(8,128)(2,1)S(1)}, bf16[32,8192]{1,0:T(8,128)(2,1)S(1)}, u32[]{:S(2)}, u32[]{:S(2)}) %collective-permute-start) | collective-permute-done | bytes 524320 | tf_op jit(solution)/shard_map/while/body/eval_jaxpr/ppermute | solution.py:37
  234.2 3.2 select_dynamic-update-slice_fusion.8
  243.7 3.0 select_dynamic-update-slice_fusion.10
  248.1 12.6 %collective-permute-done = bf16[32,8192]{1,0:T(8,128)(2,1)S(1)} collective-permute-done((bf16[32,8192]{1,0:T(8,128)(2,1)S(1)}, bf16[32,8192]{1,0:T(8,128)(2,1)S(1)}, u32[]{:S(2)}, u32[]{:S(2)}) %collective-permute-start) | collective-permute-done | bytes 524320 | tf_op jit(solution)/shard_map/while/body/eval_jaxpr/ppermute | solution.py:37
  261.0 3.2 select_dynamic-update-slice_fusion.8
  270.5 3.0 select_dynamic-update-slice_fusion.10
  274.8 11.7 %collective-permute-done = bf16[32,8192]{1,0:T(8,128)(2,1)S(1)} collective-permute-done((bf16[32,8192]{1,0:T(8,128)(2,1)S(1)}, bf16[32,8192]{1,0:T(8,128)(2,1)S(1)}, u32[]{:S(2)}, u32[]{:S(2)}) %collective-permute-start) | collective-permute-done | bytes 524320 | tf_op jit(solution)/shard_map/while/body/eval_jaxpr/ppermute | solution.py:37
  286.8 3.2 select_dynamic-update-slice_fusion.8
  296.4 3.0 select_dynamic-update-slice_fusion.10
  300.7 10.7 %collective-permute-done = bf16[32,8192]{1,0:T(8,128)(2,1)S(1)} collective-permute-done((bf16[32,8192]{1,0:T(8,128)(2,1)S(1)}, bf16[32,8192]{1,0:T(8,128)(2,1)S(1)}, u32[]{:S(2)}, u32[]{:S(2)}) %collective-permute-start) | collective-permute-done | bytes 524320 | tf_op jit(solution)/shard_map/while/body/eval_jaxpr/ppermute | solution.py:37
  311.4 5.0 %convolution_convert_fusion.1 = bf16[8192,256]{0,1:T(8,128)(2,1)} fusion(bf16[128,8192]{1,0:T(8,128)(2,1)} %get-tuple-element.369, bf16[128,256]{1,0:T(8,128)(2,1)S(1)} %get-tuple-element.370), kind=kOutput, calls=%fused_computation.36 | convolution fusion | flops 538968064 | bytes 6356992 | tf_op jit(solution)/shard_map/td,tr->dr/dot_general | solution.py:115
  316.4 3.2 convolution_convert_fusion
  319.6 7.7 %pad_maximum_fusion = bf16[8192,512]{0,1:T(8,128)(2,1)} fusion(bf16[8192,256]{0,1:T(8,128)(2,1)} %convolution_convert_fusion, bf16[8192,256]{0,1:T(8,128)(2,1)} %convolution_convert_fusion.1), kind=kLoop, calls=%fused_computation.37 | loop fusion | flops 16777216 | bytes 16777216 | tf_op jit(solution)/shard_map/concatenate | solution.py:118
  329.2 59.5 %all-reduce = f32[8192]{0:T(1024)S(1)} all-reduce(f32[8192]{0:T(1024)S(1)} %get-tuple-element.373), channel_id=4, replica_groups=mesh['section'=2,'dp'=16] {'dp'}, use_global_device_ids=true, to_apply=%region_6.7.clone | all-reduce | flops 8192 | bytes 65536
  389.4 41.4 %reduce-scatter.2.cloned.1.call-done = bf16[512,512]{0,1:T(8,128)(2,1)} async-done(((bf16[8192,512]{0,1:T(8,128)(2,1)}), bf16[512,512]{0,1:T(8,128)(2,1)}) %reduce-scatter.2.cloned.1.call-update) | async-done | bytes 524304 | tf_op jit(solution)/shard_map/reduce_scatter | solution.py:117
  (106 shorter events, 64.3 us)
Async XLA Ops:
  7.2 165.8 %all-gather.3.cloned.1.call-start = ((), (), s32[]{:S(2)}) async-start(), calls=%async_computation.2 | async-start | bytes 4456448 | tf_op jit(solution)/shard_map/all_gather | solution.py:53
  7.9 422.8 %reduce-scatter.2.cloned.1.call-start = ((), (), s32[]{:S(2)}) async-start(), calls=%async_computation.1 | async-start | bytes 8912896 | tf_op jit(solution)/shard_map/reduce_scatter | solution.py:117
  7.9 1.9 collective-permute-start.1
  11.0 18.0 %collective-permute-start.2 = (bf16[2,512,256]{2,1,0:T(8,128)(2,1)S(1)}, bf16[2,512,256]{2,1,0:T(8,128)(2,1)S(1)}, u32[]{:S(2)}, u32[]{:S(2)}) collective-permute-start(bf16[2,512,256]{2,1,0:T(8,128)(2,1)S(1)} %get-tuple-element.479), channel_id=1, source_target_pairs={{0,2},{1,3},{2,0},{3,1},{4,6},{5,7},{6,4},{7,5},{8,10},{9,11},{10,... | collective-permute-start | bytes 1572872 | tf_op jit(solution)/shard_map/ppermute | solution.py:23
  29.3 45.1 %collective-permute-start.3 = (bf16[4,512,256]{2,1,0:T(8,128)(2,1)S(1)}, bf16[4,512,256]{2,1,0:T(8,128)(2,1)S(1)}, u32[]{:S(2)}, u32[]{:S(2)}) collective-permute-start(bf16[4,512,256]{2,1,0:T(8,128)(2,1)S(1)} %bitcast.57), channel_id=1, source_target_pairs={{0,4},{1,5},{2,6},{3,7},{4,0},{5,1},{6,2},{7,3},{8,12},{9,13},{10,... | collective-permute-start | bytes 3145736 | tf_op jit(solution)/shard_map/ppermute | solution.py:23
  75.0 93.0 %collective-permute-start.4 = (bf16[8,512,256]{2,1,0:T(8,128)(2,1)S(1)}, bf16[8,512,256]{2,1,0:T(8,128)(2,1)}, u32[]{:S(2)}, u32[]{:S(2)}) collective-permute-start(bf16[8,512,256]{2,1,0:T(8,128)(2,1)S(1)} %bitcast.52), channel_id=1, source_target_pairs={{0,8},{1,9},{2,10},{3,11},{4,12},{5,13},{6,14},{7,15},{8,0},{9,1},... | collective-permute-start | bytes 6291464 | tf_op jit(solution)/shard_map/ppermute | solution.py:23
  174.5 3.0 copy-start.2
  174.5 3.0 copy-start.4
  174.5 3.0 copy-start.5
  177.9 3.5 copy-start
  183.8 2.2 copy-start.1
  190.5 15.7 %collective-permute-start = (bf16[32,8192]{1,0:T(8,128)(2,1)S(1)}, bf16[32,8192]{1,0:T(8,128)(2,1)S(1)}, u32[]{:S(2)}, u32[]{:S(2)}) collective-permute-start(bf16[32,8192]{1,0:T(8,128)(2,1)S(1)} %get-tuple-element.592), channel_id=1, source_target_pairs={{16,0},{17,1},{18,2},{19,3},{20,4},{21,5},{22,6},{23,7},{24,8},{25... | collective-permute-start | bytes 1572872 | tf_op jit(solution)/shard_map/while/body/eval_jaxpr/ppermute | solution.py:37
  206.5 3.5 copy-start
  212.4 2.2 copy-start.1
  219.0 14.8 %collective-permute-start = (bf16[32,8192]{1,0:T(8,128)(2,1)S(1)}, bf16[32,8192]{1,0:T(8,128)(2,1)S(1)}, u32[]{:S(2)}, u32[]{:S(2)}) collective-permute-start(bf16[32,8192]{1,0:T(8,128)(2,1)S(1)} %get-tuple-element.592), channel_id=1, source_target_pairs={{16,0},{17,1},{18,2},{19,3},{20,4},{21,5},{22,6},{23,7},{24,8},{25... | collective-permute-start | bytes 1572872 | tf_op jit(solution)/shard_map/while/body/eval_jaxpr/ppermute | solution.py:37
  234.2 3.5 copy-start
  240.1 2.2 copy-start.1
  246.7 13.9 %collective-permute-start = (bf16[32,8192]{1,0:T(8,128)(2,1)S(1)}, bf16[32,8192]{1,0:T(8,128)(2,1)S(1)}, u32[]{:S(2)}, u32[]{:S(2)}) collective-permute-start(bf16[32,8192]{1,0:T(8,128)(2,1)S(1)} %get-tuple-element.592), channel_id=1, source_target_pairs={{16,0},{17,1},{18,2},{19,3},{20,4},{21,5},{22,6},{23,7},{24,8},{25... | collective-permute-start | bytes 1572872 | tf_op jit(solution)/shard_map/while/body/eval_jaxpr/ppermute | solution.py:37
  261.0 3.5 copy-start
  273.5 13.0 %collective-permute-start = (bf16[32,8192]{1,0:T(8,128)(2,1)S(1)}, bf16[32,8192]{1,0:T(8,128)(2,1)S(1)}, u32[]{:S(2)}, u32[]{:S(2)}) collective-permute-start(bf16[32,8192]{1,0:T(8,128)(2,1)S(1)} %get-tuple-element.592), channel_id=1, source_target_pairs={{16,0},{17,1},{18,2},{19,3},{20,4},{21,5},{22,6},{23,7},{24,8},{25... | collective-permute-start | bytes 1572872 | tf_op jit(solution)/shard_map/while/body/eval_jaxpr/ppermute | solution.py:37
  286.8 3.5 copy-start
  292.7 2.2 copy-start.1
  299.4 12.1 %collective-permute-start = (bf16[32,8192]{1,0:T(8,128)(2,1)S(1)}, bf16[32,8192]{1,0:T(8,128)(2,1)S(1)}, u32[]{:S(2)}, u32[]{:S(2)}) collective-permute-start(bf16[32,8192]{1,0:T(8,128)(2,1)S(1)} %get-tuple-element.592), channel_id=1, source_target_pairs={{16,0},{17,1},{18,2},{19,3},{20,4},{21,5},{22,6},{23,7},{24,8},{25... | collective-permute-start | bytes 1572872 | tf_op jit(solution)/shard_map/while/body/eval_jaxpr/ppermute | solution.py:37
  311.4 5.0 %copy-start.3 = (bf16[128,8192]{1,0:T(8,128)(2,1)S(1)}, bf16[128,8192]{1,0:T(8,128)(2,1)}, u32[]{:S(2)}) copy-start(bf16[128,8192]{1,0:T(8,128)(2,1)} %get-tuple-element.371) | copy-start | bytes 6291460
  (2 other events, 2.8 us)
Sparse Core Ops, SparseCore 0:
  10.2 64.7 all-gather.2
  327.5 103.2 reduce-scatter.1
